TPU v7x, 32 devices: a whole 2x2x4 slice. The times are simulated.
32 devices in a mesh: groups: 2 (over y), tensor: 16 (over z, x, core).
Axes of the slice: x: 2, y: 2, z: 4, core: 2. Of those that a mesh axis runs over, the one named last changes fastest.
Arguments:
- normed_input: bfloat16 [16, 2, 8192], P('groups', None, 'tensor'), parts along dimension 0, may hold values from -6 to 6
- query_weight: bfloat16 [8192, 8192], P('tensor'), may hold values from -0.0625 to 0.0625
- query_gain: float32 [128], replicated, may hold values from 0.5 to 50
- image_cache: bfloat16 [32, 1601, 2048], P(('groups', 'tensor')), parts along dimension 0, may hold values from -18 to 18
- tile_count: int32 [16], P('groups'), parts along dimension 0, may hold values from 1 to 4, as said below
- image_first_slot: int32 [16], P('groups'), parts along dimension 0, may hold values from 0 to 15, as said below
- cross_tile_mask: int32 [16, 2, 4], P('groups'), parts along dimension 0, may hold values 0 or 1
- output_weight: bfloat16 [8192, 8192], P(None, 'tensor'), may hold values from -0.0625 to 0.0625
- output_gate: float32 [1], replicated, may hold values from 0.3 to 1.5
Outputs:
- cross_output: bfloat16 [16, 2, 8192], P('groups', None, 'tensor'), parts along dimension 0
There are 2 independent parts, one for each index of `groups`. A program takes and returns all parts, laid end to end along the dimension named above; an argument that names none is the same for every part. Nothing has to cross between parts.
Inputs may be any that keep to these rules, and one draw needn't show every extreme that they name: tile_count sums to 16; some row has 4 tiles. Row r's tiles are pool slots image_first_slot[r] to image_first_slot[r] + tile_count[r] - 1; the images fill all 16 slots, each slot belonging to exactly one row.
All inputs are finite; a program needn't handle non-finite values.
Results may differ from a plain program's by a relative error of at most 0.0077.
Values may be sent and summed in bfloat16 or wider, within the bound.
A program may use at most 64 MiB of HBM per device.

v0:
```python
import math

import jax
import jax.numpy as jnp
from jax import lax
from jax.sharding import PartitionSpec as P

EPSILON = 1e-05
NEGATIVE_FLOOR = -1e30


def membership(image_first_slot, tile_count, pool_slots):
    ends = image_first_slot + tile_count
    return (pool_slots[:, None] >= image_first_slot[None, :]) & (
        pool_slots[:, None] < ends[None, :]
    )


def active_status(member_flag, image_first_slot, cross_tile_mask, pool_slots):
    member_int = member_flag.astype(jnp.int32)
    tile_index = jnp.sum(member_int * (pool_slots[:, None] - image_first_slot[None, :]), axis=1)
    row_masks = jnp.sum(member_int[:, :, None, None] * cross_tile_mask[None], axis=1)
    positions = jnp.arange(cross_tile_mask.shape[2], dtype=jnp.int32)
    chosen = jnp.sum(
        jnp.where(positions[None, None, :] == tile_index[:, None, None], row_masks, 0), axis=2
    )
    return (tile_index[:, None] == 0) | (chosen == 1)


def tile_partial(query_rows, cache_tile, head_size):
    steps = query_rows.shape[0]
    kv_width = cache_tile.shape[1] // 2
    kv_heads = kv_width // head_size
    group = query_rows.shape[1] // kv_width
    grouped = query_rows.reshape(steps, kv_heads, group, head_size)
    keys = cache_tile[:, :kv_width].reshape(-1, kv_heads, head_size)
    values = cache_tile[:, kv_width:].reshape(-1, kv_heads, head_size)
    scores = jnp.einsum("skgd,tkd->skgt", grouped, keys, preferred_element_type=jnp.float32) * (
        1.0 / math.sqrt(head_size)
    )
    tops = jnp.max(scores, axis=3)
    weights = jnp.exp(scores - tops[..., None]).astype(jnp.bfloat16)
    totals = jnp.sum(weights.astype(jnp.float32), axis=3)
    mixed = jnp.einsum("skgt,tkd->skgd", weights, values, preferred_element_type=jnp.float32)
    return (tops.reshape(steps, -1), totals.reshape(steps, -1), mixed.reshape(steps, -1))


def finish(numer_pairs, denom_pairs, head_size):
    pairs = numer_pairs.shape[0]
    heads = denom_pairs.shape[1]
    shaped = numer_pairs.reshape(pairs, heads, head_size) / denom_pairs[..., None]
    return shaped.astype(jnp.bfloat16).reshape(pairs, heads * head_size)


def body(
    normed_input,
    query_weight,
    query_gain,
    image_cache,
    tile_count,
    image_first_slot,
    cross_tile_mask,
    output_weight,
    output_gate,
):
    rows, steps, local_width = normed_input.shape
    head_size = query_gain.shape[0]
    heads = query_weight.shape[1] // head_size
    slot_count = image_cache.shape[0]
    flattened = normed_input.reshape(rows * steps, local_width)
    query = lax.psum_scatter(
        jnp.dot(flattened, query_weight, preferred_element_type=jnp.float32),
        "tensor",
        scatter_dimension=0,
        tiled=True,
    )
    shaped = query.reshape(slot_count, heads, head_size)
    normed = (
        shaped * lax.rsqrt(jnp.mean(shaped * shaped, axis=2, keepdims=True) + EPSILON) * query_gain
    )
    normed = normed.astype(jnp.bfloat16).reshape(slot_count, heads * head_size)
    all_queries = lax.all_gather(normed, "tensor", axis=0, tiled=True)
    target_device = lax.axis_index("tensor")
    pool_slots = target_device * slot_count + jnp.arange(slot_count, dtype=jnp.int32)
    member_flag = membership(image_first_slot, tile_count, pool_slots)
    active_entry = active_status(member_flag, image_first_slot, cross_tile_mask, pool_slots)
    by_row = all_queries.reshape(rows, steps * heads * head_size)
    selected = jnp.dot(member_flag.astype(jnp.bfloat16), by_row, preferred_element_type=jnp.float32)
    selected = selected.astype(jnp.bfloat16).reshape(slot_count, steps, heads * head_size)

    def slot_term(operands):
        return tile_partial(operands[0], operands[1], head_size)

    tops, totals, mixed = lax.map(slot_term, (selected, image_cache))
    masked = jnp.where(active_entry[:, :, None], tops, NEGATIVE_FLOOR)
    pair_index = target_device * slot_count + jnp.arange(slot_count, dtype=jnp.int32)
    pair_row = pair_index // steps
    pair_step = pair_index % steps
    gathered_tops, gathered_totals, gathered_mixed = (
        lax.all_gather(masked, "tensor", axis=0, tiled=True),
        lax.all_gather(totals, "tensor", axis=0, tiled=True),
        lax.all_gather(mixed, "tensor", axis=0, tiled=True),
    )
    all_slots = gathered_tops.shape[0]
    every_slot = jnp.arange(all_slots, dtype=jnp.int32)
    full_member = membership(image_first_slot, tile_count, every_slot)
    slot_pick = full_member[:, pair_row]
    step_pick = jnp.arange(steps, dtype=jnp.int32)[None, :] == pair_step[:, None]
    chosen = slot_pick[:, :, None] & step_pick[None, :, :]
    spread = jnp.where(chosen[..., None], gathered_tops[:, None, :, :], NEGATIVE_FLOOR)
    pair_max = jnp.max(spread, axis=(0, 2))
    weights = jnp.where(chosen[..., None], jnp.exp(spread - pair_max[None, :, None, :]), 0.0)
    denom_pairs = jnp.sum(weights * gathered_totals[:, None, :, :], axis=(0, 2))
    mixed_heads = gathered_mixed.reshape(all_slots, steps, heads, head_size)
    numer_pairs = jnp.einsum(
        "spth,sthd->phd", weights, mixed_heads, precision=lax.Precision.HIGHEST
    )
    numer_pairs = numer_pairs.reshape(slot_count, heads * head_size)
    attended = finish(numer_pairs, denom_pairs, head_size)
    projected = jnp.dot(
        lax.all_gather(attended, "tensor", axis=0, tiled=True),
        output_weight,
        preferred_element_type=jnp.float32,
    )
    result = jnp.tanh(output_gate[0]) * projected
    return result.astype(jnp.bfloat16).reshape(rows, steps, -1)


def solution(mesh):
    return jax.shard_map(
        body,
        mesh=mesh,
        in_specs=(
            P("groups", None, "tensor"),
            P("tensor", None),
            P(),
            P(("groups", "tensor"), None, None),
            P("groups"),
            P("groups"),
            P("groups", None, None),
            P(None, "tensor"),
            P(),
        ),
        out_specs=P("groups", None, "tensor"),
        check_vma=False,
    )
```

profile of v0, /device:TPU:1, one launch (start us, length us, event | category | flops | bytes accessed | tf_op | source)
XLA Modules:
  0.0 217.0 jit_solution(3710583259249691234)
XLA Ops:
  6.5 0.7 reshape.264
  7.3 5.4 %fusion.27 = f32[16,8192]{1,0:T(8,128)} fusion(bf16[16,512]{1,0:T(8,128)(2,1)S(1)} %reshape.264, bf16[512,8192]{1,0:T(8,128)(2,1)} %param.10), kind=kOutput, calls=%fused_computation.45 | convolution fusion | flops 134217728 | bytes 8929280 | tf_op jit(solution)/shard_map/dot_general | solution.py:72
  12.6 0.0 all-reduce.3.cloned.1.call-update
  12.7 0.0 all-gather.4.cloned.1.call-start
  12.7 3.7 %fusion.25 = (bf16[1601,1024]{1,0:T(8,128)(2,1)S(1)}, bf16[1601,1024]{1,0:T(8,128)(2,1)S(1)}) fusion(bf16[1601,2048]{1,0:T(8,128)(2,1)} %bitcast.51), kind=kLoop, calls=%fused_computation.43 | loop fusion | bytes 13115392 | tf_op jit(solution)/shard_map/while/body/eval_jaxpr/slice | solution.py:37
  16.4 0.9 copy.38
  17.3 0.3 slice_bitcast_fusion.1
  17.6 0.9 copy.39
  18.4 0.0 copy-start.6
  18.4 0.0 copy-start.2
  18.5 1.8 slice_bitcast_fusion
  20.3 0.6 dynamic-slice.4
  20.9 0.6 select_reduce_fusion.1
  21.5 84.6 %all-reduce.3.cloned.1.call-done = f32[16,8192]{1,0:T(8,128)} async-done(((f32[16,8192]{1,0:T(8,128)}), f32[16,8192]{1,0:T(8,128)}) %all-reduce.3.cloned.1.call-update) | async-done | bytes 524304
  106.1 1.6 dynamic-slice_multiply_fusion
  107.8 0.1 reduce_sum.55
  107.9 0.1 mul.75
  108.0 1.7 convert_bitcast_fusion
  109.6 23.6 %all-gather = bf16[16,1,8192]{2,1,0:T(2,128)(2,1)} all-gather(bf16[1,1,8192]{2,1,0:T(2,128)(2,1)S(1)} %convert_bitcast_fusion), channel_id=1, replica_groups=mesh['groups'=2,'tensor'=16] {'tensor'}, dimensions={0}, use_global_device_ids=true | all-gather | bytes 278528 | tf_op jit(solution)/shard_map/all_gather | solution.py:82
  133.2 3.2 %reduce.12 = bf16[16,8192]{1,0:T(8,128)(2,1)} reduce(bf16[16,1,8192]{2,1,0:T(2,128)(2,1)} %all-gather, bf16[]{:T(256)} %constant.103), dimensions={1}, to_apply=%all-gather.reduce_sub_computation | reduce | bytes 524290 | tf_op jit(solution)/shard_map/all_gather | solution.py:82
  136.5 1.1 reshape.265
  137.5 0.2 fusion.21
  137.7 1.1 fusion.26
  138.9 0.6 copy-done
  139.4 1.2 fusion.10
  140.7 0.7 broadcast_in_dim.87
  141.3 0.0 all-gather.4.cloned.1.call-update
  141.4 0.6 iota_compare_fusion.2
  143.2 0.1 fusion.20
  143.3 0.1 multiply_reduce_fusion.1
  143.5 0.1 select_reduce_fusion
  143.6 0.1 broadcast_and_fusion
  143.7 1.4 convert_reduce_fusion
  145.1 0.1 broadcast_in_dim.97
  145.2 0.1 broadcast_in_dim.93
  145.3 17.5 %all_gather.18 = f32[16,2,64]{2,1,0:T(2,128)S(1)} all-gather(f32[1,2,64]{2,1,0:T(2,128)S(1)} %broadcast_in_dim.97), channel_id=1, replica_groups=mesh['groups'=2,'tensor'=16] {'tensor'}, dimensions={0}, use_global_device_ids=true | all-gather | bytes 8704 | tf_op jit(solution)/shard_map/all_gather | solution.py:101
  162.7 0.1 broadcast_select_fusion.1
  162.8 19.0 %all_gather.17 = f32[16,2,64]{2,1,0:T(2,128)S(1)} all-gather(f32[1,2,64]{2,1,0:T(2,128)S(1)} %broadcast_select_fusion.1), channel_id=1, replica_groups=mesh['groups'=2,'tensor'=16] {'tensor'}, dimensions={0}, use_global_device_ids=true | all-gather | bytes 8704 | tf_op jit(solution)/shard_map/all_gather | solution.py:100
  181.8 0.1 fusion.19
  181.9 0.1 multiply_reduce_fusion
  182.0 0.1 copy.31
  182.1 0.0 all-gather.4.cloned.1.call-done
  182.1 2.1 reshape.269
  184.2 1.7 fusion.14
  185.9 0.1 divide_convert_fusion
  186.1 18.9 %all-gather.1 = bf16[16,1,8192]{2,1,0:T(2,128)(2,1)S(1)} all-gather(bf16[1,1,8192]{2,1,0:T(2,128)(2,1)S(1)} %reshape.298), channel_id=1, replica_groups=mesh['groups'=2,'tensor'=16] {'tensor'}, dimensions={0}, use_global_device_ids=true | all-gather | bytes 278528 | tf_op jit(solution)/shard_map/all_gather | solution.py:121
  204.9 4.6 %fusion.13 = bf16[16,512]{1,0:T(8,128)(2,1)S(1)} fusion(bf16[8192,512]{1,0:T(8,128)(2,1)} %param.16, bf16[16,1,8192]{2,1,0:T(2,128)(2,1)S(1)} %all-gather.1, f32[]{:T(128)} %bitcast), kind=kOutput, calls=%fused_computation.10 | convolution fusion | flops 134234112 | bytes 8667140 | tf_op jit(solution)/shard_map/dot_general | solution.py:120
  209.6 0.6 reshape.271
  (23 shorter events, 0.1 us)
Async XLA Ops:
  6.5 99.6 %all-reduce.3.cloned.1.call-start = ((), (), s32[]{:S(2)}) async-start(), calls=%async_computation.1 | async-start | bytes 1048576
  12.7 169.4 %all-gather.4.cloned.1.call-start = ((), (), s32[]{:S(2)}) async-start(), calls=%async_computation | async-start | bytes 1114112 | tf_op jit(solution)/shard_map/all_gather | solution.py:102
  18.4 1.9 copy-start.6
  18.4 2.4 %copy-start.2 = (s32[8]{0:T(128)S(1)}, s32[8]{0:T(128)}, u32[]{:S(2)}) copy-start(s32[8]{0:T(128)} %param.14) | copy-start | bytes 100
  18.4 2.4 %copy-start.5 = (s32[8]{0:T(128)S(1)}, s32[8]{0:T(128)}, u32[]{:S(2)}) copy-start(s32[8]{0:T(128)} %param.13) | copy-start | bytes 100
  18.5 89.4 %copy-start.4 = (f32[128]{0:T(128)S(1)}, f32[128]{0:T(128)}, u32[]{:S(2)}) copy-start(f32[128]{0:T(128)} %param.11) | copy-start | bytes 1540
  137.5 1.9 copy-start
  138.9 1.8 copy-start.1
  138.9 4.4 %copy-start.3 = (s32[8,2,4]{0,2,1:T(4,128)S(1)}, s32[8,2,4]{0,2,1:T(4,128)}, u32[]{:S(2)}) copy-start(s32[8,2,4]{0,2,1:T(4,128)} %param.15) | copy-start | bytes 772
Sparse Core Ops, SparseCore 0:
  12.8 93.3 all-reduce.2
  141.5 34.9 all-gather.3
where the time goes:
time: 218 us; the launch traced here: 217 us
  waiting for transfers between devices  84.7 us (39%)
  blocking collectives  78.9 us (36%)
  between operations  14.9 us (7%)
  local copies, waits for them, and re-layouts  14.2 us (7%)
  matrix products  14.2 us (7%)
  other arithmetic  10.1 us (5%)
    unnamed x3, waiting for transfers between devices  84.7 us
    all_gather x1, blocking collectives, body(): all_queries = lax.all_gather(normed, 'tensor', axis=0, tiled=True)  23.6 us
    all_gather x1, blocking collectives, body(): lax.all_gather(masked, 'tensor', axis=0, tiled=True)  19 us
    all_gather x1, blocking collectives, body(): lax.all_gather(attended, 'tensor', axis=0, tiled=True)  18.9 us
    all_gather x1, blocking collectives, body(): lax.all_gather(totals, 'tensor', axis=0, tiled=True)  17.5 us
    dot_general x1, matrix products, body(): jnp.dot(flattened, query_weight, preferred_element_type=jnp.float32)  5.38 us
    dot_general x1, matrix products, body(): jnp.dot(lax.all_gather(attended, 'tensor', axis=0, tiled=True), output_we...  4.62 us
  transfers between devices with their start and end apart: 2, of which 1 were waited for; matrix products, arithmetic and copies ran while one was open for 5% of the time, Pallas kernels for 0%

commit v1 on v0

--- a/solution.py
+++ b/solution.py
@@ -1,12 +1,16 @@
+import functools
 import math
 
 import jax
 import jax.numpy as jnp
 from jax import lax
+from jax.experimental import pallas as pl
+from jax.experimental.pallas import tpu as pltpu
 from jax.sharding import PartitionSpec as P
 
 EPSILON = 1e-05
 NEGATIVE_FLOOR = -1e30
+MESH = pl.DeviceIdType.MESH
 
 
 def membership(image_first_slot, tile_count, pool_slots):
@@ -126,9 +130,333 @@
     return result.astype(jnp.bfloat16).reshape(rows, steps, -1)
 
 
+def fused_kernel(
+    count_ref, first_ref, mask_ref, x_ref, gain_ref, wq_hbm, cache_hbm, wo_hbm, out_ref,
+    wq_s, kv_s, wo_s, send_a, recv_a, send_b, recv_b, send_c, recv_c, send_e, recv_e, live_s, att_s, att_all,
+    wq_sem, kv_sem, wo_sem, a_send, a_recv, b_send, b_recv, c_send, c_recv, e_send, e_recv,
+    f_send, f_recv, p_send, p_recv,
+    *, devices, kv_heads, steps, head_size,
+):
+    chips = devices // 2
+    me = lax.axis_index("tensor")
+    core = lax.rem(me, 2)
+    chip = lax.div(me, 2)
+    partner = me + 1 - 2 * core
+    pairs, _ = x_ref.shape
+    rows = pairs // steps
+    width = wq_s.shape[2]
+    local_heads = width // head_size
+    tile = local_heads * steps
+    block = rows * tile
+
+    def remote(src, dst, send_sem, recv_sem, device):
+        return pltpu.make_async_remote_copy(
+            src_ref=src, dst_ref=dst, send_sem=send_sem, recv_sem=recv_sem,
+            device_id={"tensor": device}, device_id_type=MESH,
+        )
+
+    def at(index, size):
+        return pl.ds(pl.multiple_of(index * size, size), size)
+
+    ahead = [lax.rem(chip + 1 + i, chips) for i in range(chips)]
+    behind = [lax.rem(chip + 2 * chips - 1 - i, chips) for i in range(chips)]
+    order = [2 * c + 1 - core for c in ahead] + [2 * c + core for c in ahead]
+    wq_copies = [
+        pltpu.make_async_copy(wq_hbm.at[:, at(b, width)], wq_s.at[n], wq_sem.at[n])
+        for n, b in enumerate(order)
+    ]
+    for copy in wq_copies:
+        copy.start()
+
+    barrier = pltpu.get_barrier_semaphore()
+    for j in range(1, devices):
+        pl.semaphore_signal(
+            barrier, inc=1, device_id={"tensor": lax.rem(me + j, devices)}, device_id_type=MESH
+        )
+    pl.semaphore_wait(barrier, devices - 1)
+
+    x = x_ref[...]
+    a_copies = [
+        remote(send_a.at[i], recv_a.at[i], a_send.at[i], a_recv.at[i], partner) for i in range(chips)
+    ]
+    b_copies = [
+        remote(send_b.at[i], recv_b.at[i], b_send.at[i], b_recv.at[i], 2 * ahead[i] + core)
+        for i in range(chips - 1)
+    ]
+    for i in range(chips):
+        wq_copies[i].wait()
+        send_a[i] = jnp.dot(x, wq_s[i], preferred_element_type=jnp.float32)
+        a_copies[i].start()
+    query = None
+    for i in range(chips):
+        wq_copies[chips + i].wait()
+        mine = jnp.dot(x, wq_s[chips + i], preferred_element_type=jnp.float32)
+        a_copies[i].wait_recv()
+        total = mine + recv_a[i]
+        if i < chips - 1:
+            send_b[i] = total
+            b_copies[i].start()
+        else:
+            query = total
+
+    kv_copy = pltpu.make_async_copy(cache_hbm.at[0], kv_s, kv_sem.at[0])
+    kv_copy.start()
+    wo_copy = pltpu.make_async_copy(wo_hbm, wo_s, wo_sem.at[0])
+    wo_copy.start()
+
+    shape = (devices * tile, pairs)
+    row_at = lax.broadcasted_iota(jnp.int32, shape, 0)
+    pair_at = lax.broadcasted_iota(jnp.int32, shape, 1)
+    slot_at = row_at >> (tile.bit_length() - 1)
+    inner = row_at & (tile - 1)
+    step_at = inner & (steps - 1)
+    head_at = inner >> (steps.bit_length() - 1)
+    row_of = jnp.zeros(shape, jnp.int32)
+    for r in range(rows):
+        low = first_ref[r]
+        row_of = jnp.where((slot_at >= low) & (slot_at < low + count_ref[r]), r, row_of)
+    wanted = row_of * steps + step_at == pair_at
+
+    whole = (devices, tile, head_size)
+    slot_at = lax.broadcasted_iota(jnp.int32, whole, 0)
+    step_at = lax.broadcasted_iota(jnp.int32, whole, 1) & (steps - 1)
+    live_row = jnp.full(whole, -1, jnp.int32)
+    for r in range(rows):
+        tile_at = slot_at - first_ref[r]
+        allowed = jnp.where(tile_at == 0, 1, 0)
+        for t in range(1, mask_ref.shape[1]):
+            for s in range(steps):
+                allowed = jnp.where((tile_at == t) & (step_at == s), mask_ref[s, t, r], allowed)
+        live_row = jnp.where((tile_at < count_ref[r]) & (allowed == 1), r, live_row)
+    live_s[...] = live_row
+
+    for i in range(chips - 1):
+        b_copies[i].wait_recv()
+        query = query + recv_b[i]
+    gain = gain_ref[...]
+    routed = jnp.zeros((devices * tile, head_size), jnp.float32)
+    for h in range(local_heads):
+        part = query[:, h * head_size : (h + 1) * head_size]
+        mean = jnp.mean(part * part, axis=1, keepdims=True)
+        normed = (part * lax.rsqrt(mean + EPSILON) * gain).astype(jnp.bfloat16)
+        pick = jnp.where(wanted & (head_at == h), 1.0, 0.0).astype(jnp.bfloat16)
+        routed = routed + jnp.dot(pick, normed, preferred_element_type=jnp.float32)
+    send_c[...] = routed
+    c_copies = []
+    for j in range(1, devices):
+        device = lax.rem(me + j, devices)
+        c_copies.append(
+            remote(
+                send_c.at[at(device, tile)], recv_c.at[at(me, tile)],
+                c_send.at[j], c_recv.at[j], device,
+            )
+        )
+        c_copies[-1].start()
+    recv_c[at(me, tile), :] = send_c[at(me, tile), :]
+    kv_copy.wait()
+    for copy in c_copies:
+        copy.wait_recv()
+
+    q_all = recv_c[...].astype(jnp.bfloat16)
+    group_rows = devices * tile // kv_heads
+    kv_width = kv_heads * head_size
+    lane = lax.broadcasted_iota(jnp.int32, (group_rows, head_size), 1)
+    for g in range(kv_heads):
+        keys = kv_s[:, g * head_size : (g + 1) * head_size]
+        values = kv_s[:, kv_width + g * head_size : kv_width + (g + 1) * head_size]
+        scores = lax.dot_general(
+            q_all[g * group_rows : (g + 1) * group_rows], keys, (((1,), (1,)), ((), ())),
+            preferred_element_type=jnp.float32,
+        ) * (1.0 / math.sqrt(head_size))
+        top = jnp.max(scores, axis=1, keepdims=True)
+        weights = jnp.exp(scores - top).astype(jnp.bfloat16)
+        sums = jnp.sum(weights.astype(jnp.float32), axis=1, keepdims=True)
+        mixed = jnp.dot(weights, values, preferred_element_type=jnp.float32)
+        stats = jnp.where(lane < head_size // 2, top, sums)
+        for n in range(group_rows // tile):
+            d = g * (group_rows // tile) + n
+            send_e[d, :tile, :] = mixed[n * tile : (n + 1) * tile]
+            send_e[d, tile:, :] = stats[n * tile : (n + 1) * tile]
+    e_copies = []
+    for j in range(1, devices):
+        device = lax.rem(me + j, devices)
+        e_copies.append(
+            remote(
+                send_e.at[device], recv_e.at[me], e_send.at[j], e_recv.at[j], device,
+            )
+        )
+        e_copies[-1].start()
+    recv_e[me] = send_e[me]
+    for copy in e_copies:
+        copy.wait_recv()
+
+    mixes = recv_e[:, :tile, :]
+    stats = recv_e[:, tile:, :]
+    whole = (devices, tile, head_size)
+    tops = jnp.broadcast_to(stats[:, :, 0:1], whole)
+    sums = jnp.broadcast_to(stats[:, :, head_size // 2 : head_size // 2 + 1], whole)
+    live_row = live_s[...]
+    peaks = jnp.zeros(whole, jnp.float32)
+    for r in range(rows):
+        here = live_row == r
+        peak = jnp.max(jnp.where(here, tops, NEGATIVE_FLOOR), axis=0, keepdims=True)
+        peaks = jnp.where(here, peak, peaks)
+    alive = live_row >= 0
+    factor = jnp.where(alive, jnp.exp(jnp.where(alive, tops - peaks, 0.0)), 0.0)
+    mixes = factor * mixes
+    sums = factor * sums
+    for r in range(rows):
+        here = live_row == r
+        numer = jnp.sum(jnp.where(here, mixes, 0.0), axis=0)
+        denom = jnp.sum(jnp.where(here, sums, 0.0), axis=0)
+        att_s[r * tile : (r + 1) * tile, :] = numer / denom
+
+    to = lax.broadcasted_iota(jnp.int32, (block, block), 0)
+    fro = lax.broadcasted_iota(jnp.int32, (block, block), 1)
+    to_head = to >> (pairs.bit_length() - 1)
+    to_pair = to & (pairs - 1)
+    source = (
+        (to_pair >> (steps.bit_length() - 1)) * tile + to_head * steps + (to_pair & (steps - 1))
+    )
+    swap = jnp.where(source == fro, 1.0, 0.0).astype(jnp.bfloat16)
+    att_all[at(me, block), :] = jnp.dot(
+        swap, att_s[...].astype(jnp.bfloat16), preferred_element_type=jnp.float32
+    ).astype(jnp.bfloat16)
+
+    f_copies = [
+        remote(
+            att_all.at[at(me, block)], att_all.at[at(me, block)],
+            f_send.at[i], f_recv.at[i], 2 * ahead[i] + core,
+        )
+        for i in range(chips - 1)
+    ]
+    arrived = [me] + [2 * behind[i] + core for i in range(chips - 1)]
+    p_copies = [
+        remote(
+            att_all.at[at(b, block)], att_all.at[at(b, block)], p_send.at[n], p_recv.at[n], partner
+        )
+        for n, b in enumerate(arrived)
+    ]
+    p_copies[0].start()
+    for copy in f_copies:
+        copy.start()
+    wo_copy.wait()
+
+    def projected(b):
+        heads = att_all[at(b, block), :]
+        joined = jnp.concatenate(
+            [heads[h * pairs : (h + 1) * pairs] for h in range(local_heads)], axis=1
+        )
+        return jnp.dot(joined, wo_s[at(b, width), :], preferred_element_type=jnp.float32)
+
+    result = projected(me)
+    for i in range(chips - 1):
+        f_copies[i].wait_recv()
+        p_copies[i + 1].start()
+        result = result + projected(arrived[i + 1])
+    for n in range(chips):
+        p_copies[n].wait_recv()
+        result = result + projected(arrived[n] + 1 - 2 * core)
+    out_ref[...] = result
+    for copy in a_copies + b_copies + c_copies + e_copies + f_copies + p_copies:
+        copy.wait_send()
+
+
+def fused_body(
+    devices,
+    normed_input,
+    query_weight,
+    query_gain,
+    image_cache,
+    tile_count,
+    image_first_slot,
+    cross_tile_mask,
+    output_weight,
+    output_gate,
+):
+    rows, steps, local_width = normed_input.shape
+    head_size = query_gain.shape[0]
+    tokens, cache_width = image_cache.shape[1:]
+    width = query_weight.shape[1] // devices
+    pairs = rows * steps
+    tile = width // head_size * steps
+    chips = devices // 2
+    dma = pltpu.SemaphoreType.DMA
+    smem = pl.BlockSpec(memory_space=pltpu.SMEM)
+    vmem = pl.BlockSpec(memory_space=pltpu.VMEM)
+    hbm = pl.BlockSpec(memory_space=pl.ANY)
+    result = pl.pallas_call(
+        functools.partial(
+            fused_kernel, devices=devices, kv_heads=cache_width // 2 // head_size, steps=steps,
+            head_size=head_size,
+        ),
+        out_shape=jax.ShapeDtypeStruct((pairs, output_weight.shape[1]), jnp.float32),
+        in_specs=[smem, smem, smem, vmem, vmem, hbm, hbm, hbm],
+        out_specs=vmem,
+        scratch_shapes=[
+            pltpu.VMEM((devices, local_width, width), jnp.bfloat16),
+            pltpu.VMEM((tokens, cache_width), jnp.bfloat16),
+            pltpu.VMEM(output_weight.shape, jnp.bfloat16),
+            pltpu.VMEM((chips, pairs, width), jnp.float32),
+            pltpu.VMEM((chips, pairs, width), jnp.float32),
+            pltpu.VMEM((chips - 1, pairs, width), jnp.float32),
+            pltpu.VMEM((chips - 1, pairs, width), jnp.float32),
+            pltpu.VMEM((devices * tile, head_size), jnp.float32),
+            pltpu.VMEM((devices * tile, head_size), jnp.float32),
+            pltpu.VMEM((devices, 2 * tile, head_size), jnp.float32),
+            pltpu.VMEM((devices, 2 * tile, head_size), jnp.float32),
+            pltpu.VMEM((devices, tile, head_size), jnp.int32),
+            pltpu.VMEM((rows * tile, head_size), jnp.float32),
+            pltpu.VMEM((devices * rows * tile, head_size), jnp.bfloat16),
+            dma((devices,)), dma((1,)), dma((1,)),
+            dma((chips,)), dma((chips,)), dma((chips,)), dma((chips,)),
+            dma((devices,)), dma((devices,)), dma((devices,)), dma((devices,)),
+            dma((chips,)), dma((chips,)), dma((chips,)), dma((chips,)),
+        ],
+        compiler_params=pltpu.CompilerParams(collective_id=0, has_side_effects=True),
+        name="gated_cross_attention",
+    )(
+        tile_count, image_first_slot, cross_tile_mask.transpose(1, 2, 0), normed_input.reshape(pairs, local_width),
+        query_gain.reshape(1, head_size), query_weight, image_cache, output_weight,
+    )
+    result = jnp.tanh(output_gate[0]) * result
+    return result.astype(jnp.bfloat16).reshape(rows, steps, -1)
+
+
+def power_of_two(number):
+    return number > 0 and number & (number - 1) == 0
+
+
+def fits(
+    devices, normed_input, query_weight, query_gain, image_cache, tile_count, image_first_slot,
+    cross_tile_mask, output_weight, output_gate,
+):
+    rows, steps, _ = normed_input.shape
+    head_size = query_gain.shape[0]
+    heads = query_weight.shape[1] // head_size
+    kv_heads = image_cache.shape[2] // 2 // head_size
+    if devices % 2 or heads % devices or image_cache.shape[0] != 1:
+        return False
+    tile = heads // devices * steps
+    return (
+        tile % 8 == 0
+        and head_size % 128 == 0
+        and rows * steps % 16 == 0
+        and devices % kv_heads == 0
+        and all(power_of_two(n) for n in (rows, steps, tile, devices))
+        and query_weight.size + image_cache.size + output_weight.size <= 14 * 2**20
+    )
+
+
+def chosen(devices, *arrays):
+    if fits(devices, *arrays):
+        return fused_body(devices, *arrays)
+    return body(*arrays)
+
+
 def solution(mesh):
     return jax.shard_map(
-        body,
+        functools.partial(chosen, mesh.shape["tensor"]),
         mesh=mesh,
         in_specs=(
             P("groups", None, "tensor"),

time: 218 us -> 41.5 us (0.19)
  waiting for transfers between devices: 84.7 us -> 0 us
  blocking collectives: 78.9 us -> 0 us
  Pallas kernels: 0 us -> 37.8 us
  between operations: 14.9 us -> 0.7 us
  matrix products: 14.2 us -> 0 us
  local copies, waits for them, and re-layouts: 14.2 us -> 1.96 us
  other arithmetic: 10.1 us -> 0.77 us
    unnamed x3 -> x0, waiting for transfers between devices: 84.7 us -> none
    all_gather x4 -> x0, blocking collectives: 78.9 us -> none  [the longest x1 23.6 us: body(): all_queries = lax.all_gather(normed, 'tensor', axis=0, tiled=True)]
    pallas_call x0 -> x1, Pallas kernels: none -> 37.8 us  [fused_body(): pl.pallas_call(functools.partial(fused_kernel, devices=devices, kv_heads=...]
    dot_general x6 -> x0, matrix products: 14.2 us -> none  [the longest x1 5.38 us: body(): jnp.dot(flattened, query_weight, preferred_element_type=jnp.float32)]
    reshape x6 -> x2, local copies, waits for them, and re-layouts: 6.62 us -> 1.96 us  [the longest x1 1.34 us: fused_body(): normed_input.reshape(pairs, local_width)]
    slice x1 -> x0, local copies, waits for them, and re-layouts: 3.69 us -> none  [tile_partial(): values = cache_tile[:, kv_width:].reshape(-1, kv_heads, head_size)]
    all_gather x1 -> x0, other arithmetic: 3.25 us -> none  [body(): all_queries = lax.all_gather(normed, 'tensor', axis=0, tiled=True)]
    unnamed x18 -> x0, local copies, waits for them, and re-layouts: 2.9 us -> none
  transfers between devices with their start and end apart: 2 -> 0, of which waited for: 1 -> 0; matrix products, arithmetic and copies ran while one was open for 5% -> 0% of each run, Pallas kernels for 0% -> 0%
where the time goes in v1:
time: 41.5 us; the launch traced here: 41.2 us
  Pallas kernels  37.8 us (91%)
  local copies, waits for them, and re-layouts  1.96 us (5%)
  other arithmetic  0.77 us (2%)
  between operations  0.7 us (2%)
    pallas_call x1, Pallas kernels, fused_body(): pl.pallas_call(functools.partial(fused_kernel, devices=devices, kv_heads=...  37.8 us
    reshape x1, local copies, waits for them, and re-layouts, fused_body(): normed_input.reshape(pairs, local_width)  1.34 us

profile of v1, /device:TPU:1, one launch (start us, length us, event | category | flops | bytes accessed | tf_op | source)
XLA Modules:
  0.0 41.2 jit_solution(5958709559480780462)
XLA Ops:
  0.7 1.3 %reshape.10.x_ref = bf16[16,512]{1,0:T(8,128)(2,1)} reshape(bf16[8,2,512]{2,1,0:T(2,128)(2,1)} %param.9) | data formatting | bytes 32768 | tf_op jit(solution)/shard_map/reshape | solution.py:419
  2.0 37.8 %gated_cross_attention.1 = f32[16,512]{1,0:T(8,128)} custom-call(s32[8]{0:T(128)} %count_ref.1, s32[8]{0:T(128)} %first_ref.1, s32[2,4,8]{2,1,0:T(4,128)} %bitcast.3, bf16[16,512]{1,0:T(8,128)(2,1)} %reshape.10.x_ref, f32[1,128]{1,0:T(1,128)} %bitcast.4, bf16[512,8192]{1,0:T(8,128)(2,1)} %wq_hbm.1, bf16[1,1601,2048]{2,1,0:T(8,128)(2,1)} %cache_hbm.1, ...), custom_call_target="tpu_custom_call" | custom-call | tf_op jit(solution)/shard_map/gated_cross_attention/pallas_call | solution.py:388
  39.8 0.8 %multiply_convert_fusion = bf16[16,512]{1,0:T(8,128)(2,1)S(1)} fusion(f32[16,512]{1,0:T(8,128)} %gated_cross_attention.1, f32[]{:T(128)} %bitcast), kind=kLoop, calls=%fused_computation | loop fusion | flops 16384 | bytes 49156 | tf_op jit(solution)/shard_map/convert_element_type | solution.py:423
  40.6 0.6 %reshape.12 = bf16[8,2,512]{2,1,0:T(2,128)(2,1)} reshape(bf16[16,512]{1,0:T(8,128)(2,1)S(1)} %multiply_convert_fusion) | data formatting | bytes 32768 | tf_op jit(solution)/shard_map/reshape | solution.py:423

commit v2 on v1

--- a/solution.py
+++ b/solution.py
@@ -131,9 +131,9 @@
 
 
 def fused_kernel(
-    count_ref, first_ref, mask_ref, x_ref, gain_ref, wq_hbm, cache_hbm, wo_hbm, out_ref,
-    wq_s, kv_s, wo_s, send_a, recv_a, send_b, recv_b, send_c, recv_c, send_e, recv_e, live_s, att_s, att_all,
-    wq_sem, kv_sem, wo_sem, a_send, a_recv, b_send, b_recv, c_send, c_recv, e_send, e_recv,
+    count_ref, first_ref, mask_ref, gate_ref, gain_ref, x_hbm, wq_hbm, cache_hbm, wo_hbm, out_ref,
+    x_s, wq_s, kv_s, wo_s, send_a, recv_a, send_b, recv_b, send_c, recv_c, send_e, recv_e, live_s, att_s, att_all,
+    x_sem, wq_sem, kv_sem, wo_sem, a_send, a_recv, b_send, b_recv, c_send, c_recv, e_send, e_recv,
     f_send, f_recv, p_send, p_recv,
     *, devices, kv_heads, steps, head_size,
 ):
@@ -142,8 +142,8 @@
     core = lax.rem(me, 2)
     chip = lax.div(me, 2)
     partner = me + 1 - 2 * core
-    pairs, _ = x_ref.shape
-    rows = pairs // steps
+    rows = x_s.shape[0]
+    pairs = rows * steps
     width = wq_s.shape[2]
     local_heads = width // head_size
     tile = local_heads * steps
@@ -158,24 +158,39 @@
     def at(index, size):
         return pl.ds(pl.multiple_of(index * size, size), size)
 
-    ahead = [lax.rem(chip + 1 + i, chips) for i in range(chips)]
-    behind = [lax.rem(chip + 2 * chips - 1 - i, chips) for i in range(chips)]
-    order = [2 * c + 1 - core for c in ahead] + [2 * c + core for c in ahead]
-    wq_copies = [
-        pltpu.make_async_copy(wq_hbm.at[:, at(b, width)], wq_s.at[n], wq_sem.at[n])
-        for n, b in enumerate(order)
-    ]
-    for copy in wq_copies:
-        copy.start()
+    def flip(index, bits, count):
+        total = 0
+        for k in range(count.bit_length() - 1):
+            bit = lax.rem(lax.div(index, 2**k), 2)
+            total = total + (1 - bit if bits >> k & 1 else bit) * 2**k
+        return total
+
+    ahead = [flip(chip, chips - 1 - i, chips) for i in range(chips)]
+    x_copy = pltpu.make_async_copy(x_hbm, x_s, x_sem.at[0])
+    x_copy.start()
+    lag = 2
+    order = []
+    for i in range(chips + lag):
+        if i < chips:
+            order.append((i, 0))
+        if i >= lag:
+            order.append((i - lag, 1))
+    wq_copies = {}
+    for i, own in order:
+        b = 2 * ahead[i] + (core if own else 1 - core)
+        n = 2 * i + own
+        wq_copies[n] = pltpu.make_async_copy(
+            wq_hbm.at[:, at(b, width)], wq_s.at[n], wq_sem.at[n]
+        )
+        wq_copies[n].start()
 
     barrier = pltpu.get_barrier_semaphore()
     for j in range(1, devices):
         pl.semaphore_signal(
-            barrier, inc=1, device_id={"tensor": lax.rem(me + j, devices)}, device_id_type=MESH
-        )
-    pl.semaphore_wait(barrier, devices - 1)
-
-    x = x_ref[...]
+            barrier, inc=1, device_id={"tensor": flip(me, j, devices)}, device_id_type=MESH
+        )
+    x_copy.wait()
+    x = x_s[...].astype(jnp.float32).reshape(pairs, x_s.shape[2]).astype(jnp.bfloat16)
     a_copies = [
         remote(send_a.at[i], recv_a.at[i], a_send.at[i], a_recv.at[i], partner) for i in range(chips)
     ]
@@ -183,39 +198,43 @@
         remote(send_b.at[i], recv_b.at[i], b_send.at[i], b_recv.at[i], 2 * ahead[i] + core)
         for i in range(chips - 1)
     ]
-    for i in range(chips):
-        wq_copies[i].wait()
-        send_a[i] = jnp.dot(x, wq_s[i], preferred_element_type=jnp.float32)
-        a_copies[i].start()
     query = None
-    for i in range(chips):
-        wq_copies[chips + i].wait()
-        mine = jnp.dot(x, wq_s[chips + i], preferred_element_type=jnp.float32)
+    for i, own in order:
+        wq_copies[2 * i + own].wait()
+        part = jnp.dot(x, wq_s[2 * i + own], preferred_element_type=jnp.float32)
+        if not own:
+            send_a[i] = part
+            if i == 0:
+                pl.semaphore_wait(barrier, devices - 1)
+            a_copies[i].start()
+            continue
         a_copies[i].wait_recv()
-        total = mine + recv_a[i]
+        part = part + recv_a[i]
         if i < chips - 1:
-            send_b[i] = total
+            send_b[i] = part
             b_copies[i].start()
         else:
-            query = total
+            query = part
 
     kv_copy = pltpu.make_async_copy(cache_hbm.at[0], kv_s, kv_sem.at[0])
     kv_copy.start()
     wo_copy = pltpu.make_async_copy(wo_hbm, wo_s, wo_sem.at[0])
     wo_copy.start()
 
-    shape = (devices * tile, pairs)
+    shape = (devices * tile, local_heads * pairs)
     row_at = lax.broadcasted_iota(jnp.int32, shape, 0)
-    pair_at = lax.broadcasted_iota(jnp.int32, shape, 1)
+    column_at = lax.broadcasted_iota(jnp.int32, shape, 1)
     slot_at = row_at >> (tile.bit_length() - 1)
     inner = row_at & (tile - 1)
-    step_at = inner & (steps - 1)
-    head_at = inner >> (steps.bit_length() - 1)
+    pair_at = column_at & (pairs - 1)
     row_of = jnp.zeros(shape, jnp.int32)
     for r in range(rows):
         low = first_ref[r]
         row_of = jnp.where((slot_at >= low) & (slot_at < low + count_ref[r]), r, row_of)
-    wanted = row_of * steps + step_at == pair_at
+    wanted = (row_of * steps + (inner & (steps - 1)) == pair_at) & (
+        inner >> (steps.bit_length() - 1) == column_at >> (pairs.bit_length() - 1)
+    )
+    pick = jnp.where(wanted, 1.0, 0.0).astype(jnp.bfloat16)
 
     whole = (devices, tile, head_size)
     slot_at = lax.broadcasted_iota(jnp.int32, whole, 0)
@@ -234,17 +253,17 @@
         b_copies[i].wait_recv()
         query = query + recv_b[i]
     gain = gain_ref[...]
-    routed = jnp.zeros((devices * tile, head_size), jnp.float32)
+    normed = []
     for h in range(local_heads):
         part = query[:, h * head_size : (h + 1) * head_size]
         mean = jnp.mean(part * part, axis=1, keepdims=True)
-        normed = (part * lax.rsqrt(mean + EPSILON) * gain).astype(jnp.bfloat16)
-        pick = jnp.where(wanted & (head_at == h), 1.0, 0.0).astype(jnp.bfloat16)
-        routed = routed + jnp.dot(pick, normed, preferred_element_type=jnp.float32)
-    send_c[...] = routed
+        normed.append((part * lax.rsqrt(mean + EPSILON) * gain).astype(jnp.bfloat16))
+    send_c[...] = jnp.dot(
+        pick, jnp.concatenate(normed, axis=0), preferred_element_type=jnp.float32
+    )
     c_copies = []
-    for j in range(1, devices):
-        device = lax.rem(me + j, devices)
+    for j in reversed(range(1, devices)):
+        device = flip(me, j, devices)
         c_copies.append(
             remote(
                 send_c.at[at(device, tile)], recv_c.at[at(me, tile)],
@@ -257,15 +276,16 @@
     for copy in c_copies:
         copy.wait_recv()
 
-    q_all = recv_c[...].astype(jnp.bfloat16)
     group_rows = devices * tile // kv_heads
     kv_width = kv_heads * head_size
     lane = lax.broadcasted_iota(jnp.int32, (group_rows, head_size), 1)
-    for g in range(kv_heads):
-        keys = kv_s[:, g * head_size : (g + 1) * head_size]
-        values = kv_s[:, kv_width + g * head_size : kv_width + (g + 1) * head_size]
+    e_copies = []
+    for i in range(chips):
+        g = ahead[i]
+        keys = kv_s[:, at(g, head_size)]
+        values = kv_s[:, at(g + kv_heads, head_size)]
         scores = lax.dot_general(
-            q_all[g * group_rows : (g + 1) * group_rows], keys, (((1,), (1,)), ((), ())),
+            recv_c[at(g, group_rows), :].astype(jnp.bfloat16), keys, (((1,), (1,)), ((), ())),
             preferred_element_type=jnp.float32,
         ) * (1.0 / math.sqrt(head_size))
         top = jnp.max(scores, axis=1, keepdims=True)
@@ -273,20 +293,21 @@
         sums = jnp.sum(weights.astype(jnp.float32), axis=1, keepdims=True)
         mixed = jnp.dot(weights, values, preferred_element_type=jnp.float32)
         stats = jnp.where(lane < head_size // 2, top, sums)
-        for n in range(group_rows // tile):
-            d = g * (group_rows // tile) + n
-            send_e[d, :tile, :] = mixed[n * tile : (n + 1) * tile]
-            send_e[d, tile:, :] = stats[n * tile : (n + 1) * tile]
-    e_copies = []
-    for j in range(1, devices):
-        device = lax.rem(me + j, devices)
-        e_copies.append(
-            remote(
-                send_e.at[device], recv_e.at[me], e_send.at[j], e_recv.at[j], device,
+        for n in range(2):
+            send_e[i, n, :tile, :] = mixed[n * tile : (n + 1) * tile]
+            send_e[i, n, tile:, :] = stats[n * tile : (n + 1) * tile]
+        for other in range(2):
+            side = 1 - core if other else core
+            if i == chips - 1 and not other:
+                recv_e[me] = send_e[i, core]
+                continue
+            e_copies.append(
+                remote(
+                    send_e.at[i, side], recv_e.at[me],
+                    e_send.at[2 * i + other], e_recv.at[2 * i + other], 2 * g + side,
+                )
             )
-        )
-        e_copies[-1].start()
-    recv_e[me] = send_e[me]
+            e_copies[-1].start()
     for copy in e_copies:
         copy.wait_recv()
 
@@ -330,7 +351,7 @@
         )
         for i in range(chips - 1)
     ]
-    arrived = [me] + [2 * behind[i] + core for i in range(chips - 1)]
+    arrived = [me] + [2 * ahead[i] + core for i in range(chips - 1)]
     p_copies = [
         remote(
             att_all.at[at(b, block)], att_all.at[at(b, block)], p_send.at[n], p_recv.at[n], partner
@@ -357,7 +378,8 @@
     for n in range(chips):
         p_copies[n].wait_recv()
         result = result + projected(arrived[n] + 1 - 2 * core)
-    out_ref[...] = result
+    gate = jnp.tanh(jnp.full((1, width), gate_ref[0], jnp.float32))
+    out_ref[...] = (gate * result).reshape(out_ref.shape).astype(out_ref.dtype)
     for copy in a_copies + b_copies + c_copies + e_copies + f_copies + p_copies:
         copy.wait_send()
 
@@ -385,15 +407,16 @@
     smem = pl.BlockSpec(memory_space=pltpu.SMEM)
     vmem = pl.BlockSpec(memory_space=pltpu.VMEM)
     hbm = pl.BlockSpec(memory_space=pl.ANY)
-    result = pl.pallas_call(
+    return pl.pallas_call(
         functools.partial(
             fused_kernel, devices=devices, kv_heads=cache_width // 2 // head_size, steps=steps,
             head_size=head_size,
         ),
-        out_shape=jax.ShapeDtypeStruct((pairs, output_weight.shape[1]), jnp.float32),
-        in_specs=[smem, smem, smem, vmem, vmem, hbm, hbm, hbm],
+        out_shape=jax.ShapeDtypeStruct((rows, steps, output_weight.shape[1]), jnp.bfloat16),
+        in_specs=[smem, smem, smem, smem, vmem, hbm, hbm, hbm, hbm],
         out_specs=vmem,
         scratch_shapes=[
+            pltpu.VMEM((rows, steps, local_width), jnp.bfloat16),
             pltpu.VMEM((devices, local_width, width), jnp.bfloat16),
             pltpu.VMEM((tokens, cache_width), jnp.bfloat16),
             pltpu.VMEM(output_weight.shape, jnp.bfloat16),
@@ -403,12 +426,12 @@
             pltpu.VMEM((chips - 1, pairs, width), jnp.float32),
             pltpu.VMEM((devices * tile, head_size), jnp.float32),
             pltpu.VMEM((devices * tile, head_size), jnp.float32),
-            pltpu.VMEM((devices, 2 * tile, head_size), jnp.float32),
+            pltpu.VMEM((chips, 2, 2 * tile, head_size), jnp.float32),
             pltpu.VMEM((devices, 2 * tile, head_size), jnp.float32),
             pltpu.VMEM((devices, tile, head_size), jnp.int32),
             pltpu.VMEM((rows * tile, head_size), jnp.float32),
             pltpu.VMEM((devices * rows * tile, head_size), jnp.bfloat16),
-            dma((devices,)), dma((1,)), dma((1,)),
+            dma((1,)), dma((devices,)), dma((1,)), dma((1,)),
             dma((chips,)), dma((chips,)), dma((chips,)), dma((chips,)),
             dma((devices,)), dma((devices,)), dma((devices,)), dma((devices,)),
             dma((chips,)), dma((chips,)), dma((chips,)), dma((chips,)),
@@ -416,11 +439,9 @@
         compiler_params=pltpu.CompilerParams(collective_id=0, has_side_effects=True),
         name="gated_cross_attention",
     )(
-        tile_count, image_first_slot, cross_tile_mask.transpose(1, 2, 0), normed_input.reshape(pairs, local_width),
-        query_gain.reshape(1, head_size), query_weight, image_cache, output_weight,
-    )
-    result = jnp.tanh(output_gate[0]) * result
-    return result.astype(jnp.bfloat16).reshape(rows, steps, -1)
+        tile_count, image_first_slot, cross_tile_mask.transpose(1, 2, 0), output_gate,
+        query_gain.reshape(1, head_size), normed_input, query_weight, image_cache, output_weight,
+    )
 
 
 def power_of_two(number):
@@ -442,7 +463,7 @@
         tile % 8 == 0
         and head_size % 128 == 0
         and rows * steps % 16 == 0
-        and devices % kv_heads == 0
+        and devices == 2 * kv_heads
         and all(power_of_two(n) for n in (rows, steps, tile, devices))
         and query_weight.size + image_cache.size + output_weight.size <= 14 * 2**20
     )

time: 41.5 us -> 38.3 us (0.923)
  Pallas kernels: 37.8 us -> 35.9 us
  other arithmetic: 0.77 us -> 0 us
  local copies, waits for them, and re-layouts: 1.96 us -> 1.34 us
    reshape x2 -> x0, local copies, waits for them, and re-layouts: 1.96 us -> none  [the longest x1 1.34 us: fused_body(): normed_input.reshape(pairs, local_width)]
    pallas_call x1, Pallas kernels: 37.8 us -> 35.9 us  [fused_body(): pl.pallas_call(functools.partial(fused_kernel, devices=devices, kv_heads=...]
    unnamed x0 -> x1, local copies, waits for them, and re-layouts: none -> 1.34 us
    convert_element_type x1 -> x0, other arithmetic: 0.77 us -> none  [fused_body(): return result.astype(jnp.bfloat16).reshape(rows, steps, -1)]
where the time goes in v2:
time: 38.3 us; the launch traced here: 37.9 us
  Pallas kernels  35.9 us (94%)
  local copies, waits for them, and re-layouts  1.34 us (3%)
  between operations  0.66 us (2%)
    pallas_call x1, Pallas kernels, fused_body(): pl.pallas_call(functools.partial(fused_kernel, devices=devices, kv_heads=...  35.9 us
    unnamed x1, local copies, waits for them, and re-layouts  1.34 us

profile of v2, /device:TPU:1, one launch (start us, length us, event | category | flops | bytes accessed | tf_op | source)
XLA Modules:
  0.0 37.9 jit_solution(18336394779914177587)
XLA Ops:
  0.7 35.9 %gated_cross_attention.1 = bf16[8,2,512]{2,1,0:T(2,128)(2,1)} custom-call(s32[8]{0:T(128)} %count_ref.1, s32[8]{0:T(128)} %first_ref.1, s32[2,4,8]{2,1,0:T(4,128)} %bitcast.2, f32[1]{0:T(128)S(6)} %copy.11.gate_ref, f32[1,128]{1,0:T(1,128)} %bitcast.3, bf16[8,2,512]{2,1,0:T(2,128)(2,1)} %x_hbm.1, bf16[512,8192]{1,0:T(8,128)(2,1)} %wq_hbm.1, ...), custom_call_target="tpu_custom_call" | custom-call | tf_op jit(solution)/shard_map/gated_cross_attention/pallas_call | solution.py:410
  36.6 1.3 %copy.12 = bf16[8,2,512]{2,1,0:T(2,128)(2,1)} copy(bf16[8,2,512]{2,1,0:T(2,128)(2,1)} %gated_cross_attention.1) | data formatting | bytes 32768
